TPU v7x, 32 devices: a whole 2x2x4 slice. The times are simulated.
32 devices in a mesh: seq: 8 (over y, x, core), dp: 4 (over z).
Axes of the slice: x: 2, y: 2, z: 4, core: 2. Of those that a mesh axis runs over, the one named last changes fastest.
Arguments:
- queries: bfloat16 [4096, 512], P('seq', 'dp'), may hold values from -40 to 40
- keys: bfloat16 [4096, 512], P('seq', 'dp'), may hold values from -40 to 40
- values: bfloat16 [4096, 512], P('seq', 'dp'), may hold values from -6 to 6
- cross_queries: bfloat16 [4096, 512], P('seq', 'dp'), may hold values from -90 to 90
- encoded: bfloat16 [64, 128, 896], P('dp'), may hold values from -6 to 6
- cross_kv_weight: bfloat16 [896, 2, 512], P(None, None, 'dp'), may hold values from -0.1875 to 0.1875
- owners: int32 [64, 2], P('seq'), may hold values from 0 to 3, all different within a row; in each aligned block of 8 rows (0 to 7, 8 to 15, ...) at most 8 rows name the same one
- tile_rows: int32 [64, 2], P('seq'), may hold values from 0 to 15
Outputs:
- attended: bfloat16 [4096, 512], P('seq', 'dp')
- crossed: bfloat16 [4096, 512], P('seq', 'dp')
Inputs may be any that keep to these rules, and one draw needn't show every extreme that they name: `owners`: the 2 entries of a row differ; in each aligned block of 8 rows (the spans of one seq index) no owner is named by more than 8 rows, a bound that some block reaches.
All inputs are finite; a program needn't handle non-finite values.
Results may differ from a plain program's by a relative error of at most 0.0083.
Values may be sent and summed in bfloat16 or wider, within the bound.
A program may use at most 128 MiB of HBM per device.

v0:
```python
import math

import jax
import jax.numpy as jnp
from jax import lax
from jax.sharding import PartitionSpec as P

NB = 2
HS = 128


masked_score = -1e30


def passed_along(x, axis, by):
    size = lax.axis_size(axis)
    pairs = [(i, i + by) for i in range(size) if 0 <= i + by < size]
    return lax.ppermute(x, axis, pairs)


def block_update(state, query_block, positions, key_block, value_block, key_start, inv_root):
    running_max, running_total, running_sum = state
    scores = (
        jnp.einsum("qhd,khd->hqk", query_block, key_block, preferred_element_type=jnp.float32)
        * inv_root
    )
    key_positions = key_start + jnp.arange(key_block.shape[0], dtype=jnp.int32)
    allowed = key_positions[None, None, :] <= positions[None, :, None]
    scores = jnp.where(allowed, scores, masked_score)
    new_max = jnp.maximum(running_max, jnp.max(scores, axis=2))
    weights = jnp.where(allowed, jnp.exp(scores - new_max[:, :, None]), 0.0)
    fading = jnp.exp(running_max - new_max)
    new_total = running_total * fading + jnp.sum(weights, axis=2)
    added = jnp.einsum(
        "hqk,khd->qhd",
        weights.astype(jnp.bfloat16),
        value_block,
        preferred_element_type=jnp.float32,
    )
    new_sum = running_sum * jnp.transpose(fading)[:, :, None] + added
    return (new_max, new_total, new_sum)


def on_device(queries, keys, values, cross_queries, encoded, cross_kv_weight, owners, tile_rows):
    inv_root = 1.0 / math.sqrt(HS)
    tokens_here = queries.shape[0]
    half_rows = tokens_here // 2
    width = queries.shape[1]
    heads_here = width // HS
    seq_place = lax.axis_index("seq")
    near_block = queries[:half_rows].reshape(half_rows, heads_here, HS)
    near_positions = seq_place * tokens_here + jnp.arange(half_rows, dtype=jnp.int32)
    far_block = queries[half_rows:]
    far_positions = seq_place * tokens_here + half_rows + jnp.arange(half_rows, dtype=jnp.int32)
    query_sets = (
        (near_block, near_positions),
        (far_block.reshape(half_rows, heads_here, HS), far_positions),
    )

    def fold_piece(carried, pieces):
        key_rows, value_rows = pieces
        piece_rows = key_rows.shape[0]
        block_rows = math.gcd(piece_rows, 512)
        block_count = piece_rows // block_rows
        key_blocks = key_rows.reshape(block_count, block_rows, heads_here, HS)
        value_blocks = value_rows.reshape(block_count, block_rows, heads_here, HS)

        def make_step(query_block, positions):

            def step_block(block_index, state):
                key_start = block_index * block_rows
                key_block = lax.dynamic_index_in_dim(key_blocks, block_index, 0, keepdims=False)
                value_block = lax.dynamic_index_in_dim(value_blocks, block_index, 0, keepdims=False)
                return block_update(
                    state, query_block, positions, key_block, value_block, key_start, inv_root
                )

            return step_block

        updated = []
        for state, query_set in zip(carried, query_sets):
            updated.append(
                lax.fori_loop(0, block_count, make_step(query_set[0], query_set[1]), state)
            )
        return tuple(updated)

    empty_state = (
        jnp.full((heads_here, half_rows), masked_score, jnp.float32),
        jnp.zeros((heads_here, half_rows), jnp.float32),
        jnp.zeros((half_rows, heads_here, HS), jnp.float32),
    )
    final_states = fold_piece(
        (empty_state, empty_state),
        (
            lax.all_gather(keys, "seq", axis=0, tiled=True),
            lax.all_gather(values, "seq", axis=0, tiled=True),
        ),
    )
    half_outs = []
    for state in final_states:
        normed = state[2] / jnp.transpose(state[1])[:, :, None]
        half_outs.append(normed.reshape(half_rows, width).astype(jnp.bfloat16))
    near_out = half_outs[0]
    far_out = half_outs[1]
    attended = jnp.concatenate([near_out, far_out], axis=0)
    dp_count = lax.axis_size("dp")
    dp_place = lax.axis_index("dp")
    owner_flat = owners.reshape(-1)
    row_flat = tile_rows.reshape(-1)
    requests = owner_flat.shape[0]
    spans_here = owners.shape[0]
    pool_here = encoded.shape[0]
    per_place = (requests + dp_count - 1) // dp_count
    padded_requests = per_place * dp_count
    request_ids = jnp.arange(padded_requests, dtype=jnp.int32)
    live = request_ids < requests
    owner_long = jnp.concatenate(
        [owner_flat, jnp.full((padded_requests - requests,), -1, jnp.int32)]
    )
    row_long = jnp.concatenate([row_flat, jnp.zeros((padded_requests - requests,), jnp.int32)])
    chooser = (
        (live & (owner_long == dp_place))[:, None]
        & (row_long[:, None] == jnp.arange(pool_here, dtype=jnp.int32)[None, :])
    ).astype(jnp.bfloat16)
    spread_terms = jnp.einsum("rp,pjn->rjn", chooser, encoded, preferred_element_type=jnp.float32)
    my_tiles = lax.psum_scatter(
        spread_terms.astype(jnp.bfloat16), "dp", scatter_dimension=0, tiled=True
    )
    joined = lax.all_gather(my_tiles, "dp", axis=0, tiled=True)
    tile_len = encoded.shape[1]
    projected = jnp.dot(
        joined.reshape(requests * tile_len, encoded.shape[2]),
        cross_kv_weight.reshape(cross_kv_weight.shape[0], 2 * width),
        preferred_element_type=jnp.float32,
    ).astype(jnp.bfloat16)
    own_kv = projected.reshape(spans_here, NB * tile_len, 2, heads_here, HS)
    before_kv = passed_along(own_kv[-1], "seq", 1)
    every_kv = jnp.concatenate([before_kv[None], own_kv], axis=0)
    cross_keys = every_kv[:, :, 0]
    cross_values = every_kv[:, :, 1]
    span_len = tokens_here // spans_here
    padded = jnp.concatenate(
        [
            jnp.zeros((1, width), jnp.bfloat16),
            cross_queries,
            jnp.zeros((span_len - 1, width), jnp.bfloat16),
        ],
        axis=0,
    )
    span_queries = padded.reshape(spans_here + 1, span_len, heads_here, HS)
    cross_scores = (
        jnp.einsum("bqhd,bkhd->bhqk", span_queries, cross_keys, preferred_element_type=jnp.float32)
        * inv_root
    )
    row_max = jnp.max(cross_scores, axis=3, keepdims=True)
    expo = jnp.exp(cross_scores - row_max)
    cross_total = jnp.sum(expo, axis=3)
    summed = jnp.einsum(
        "bhqk,bkhd->bqhd",
        expo.astype(jnp.bfloat16),
        cross_values,
        preferred_element_type=jnp.float32,
    )
    result = summed / jnp.transpose(cross_total, (0, 2, 1))[:, :, :, None]
    crossed = result.reshape((spans_here + 1) * span_len, width)[1 : tokens_here + 1].astype(
        jnp.bfloat16
    )
    return (attended, crossed)


def solution(mesh):
    placed = (
        P("seq", "dp"),
        P("seq", "dp"),
        P("seq", "dp"),
        P("seq", "dp"),
        P("dp", None, None),
        P(None, None, "dp"),
        P("seq", None),
        P("seq", None),
    )
    return jax.shard_map(
        on_device,
        mesh=mesh,
        in_specs=placed,
        out_specs=(P("seq", "dp"), P("seq", "dp")),
        check_vma=False,
    )
```

profile of v0, /device:TPU:1, one launch (start us, length us, event | category | flops | bytes accessed | tf_op | source)
XLA Modules:
  0.0 181.2 jit_solution(5921174176498981858)
XLA Ops:
  8.8 0.7 all-gather.6.cloned.1.call-update
  9.5 0.7 broadcast_compare_fusion
  10.4 0.8 copy.36
  11.3 4.5 %fusion.48 = bf16[16,128,896]{2,0,1:T(8,128)(2,1)S(1)} fusion(bf16[16,128,896]{2,1,0:T(8,128)(2,1)} %param.16, s32[16]{0:T(128)S(1)} %eq.31, pred[16]{0:T(512)(128)(4,1)S(1)} %compare_and_fusion), kind=kOutput, calls=%fused_computation.63 | convolution fusion | flops 60555776 | bytes 7340112 | tf_op jit(solution)/shard_map/rp,pjn->rjn/dot_general | solution.py:125
  15.7 2.6 %copy.38 = bf16[16,128,896]{2,1,0:T(8,128)(2,1)} copy(bf16[16,128,896]{2,0,1:T(8,128)(2,1)S(1)} %fusion.48) | data formatting | bytes 7340032 | tf_op jit(solution)/shard_map/convert_element_type | solution.py:127
  18.5 0.8 copy-done
  19.6 16.9 %all-gather.4.cloned.1.call-done = bf16[4096,128]{1,0:T(8,128)(2,1)} async-done(((bf16[512,128]{1,0:T(8,128)(2,1)}), bf16[4096,128]{1,0:T(8,128)(2,1)}) %all-gather.4.cloned.1.call-update) | async-done | bytes 1048592 | tf_op jit(solution)/shard_map/all_gather | solution.py:95
  36.6 25.3 %all-gather.6.cloned.1.call-done = bf16[4096,128]{1,0:T(8,128)(2,1)} async-done(((bf16[512,128]{1,0:T(8,128)(2,1)}), bf16[4096,128]{1,0:T(8,128)(2,1)}) %all-gather.6.cloned.1.call-update) | async-done | bytes 1048592 | tf_op jit(solution)/shard_map/all_gather | solution.py:96
  61.8 21.1 %while.37 = (s32[]{:T(128)}, f32[1,256]{1,0:T(1,128)S(1)}, f32[1,256]{1,0:T(1,128)S(1)}, f32[256,1,128]{0,2,1:T(8,128)S(1)}, bf16[8,512,1,128]{3,1,2,0:T(8,128)(...) while((s32[]{:T(128)}, f32[1,256]{1,0:T(1,128)S(1)}, ...), condition=%wide.region_7.8_spmd.clone, body=%wide.region_4.7_spmd.clone.sunk | while | flops 68782080 | bytes 2192525 | solution.py:83
  61.9 1.2 fusion.102
  63.2 1.2 fusion.106
  64.5 1.2 fusion.102
  65.9 1.2 fusion.106
  67.1 1.2 fusion.102
  68.5 1.2 fusion.106
  69.8 1.2 fusion.102
  71.1 1.2 fusion.106
  72.4 1.2 fusion.102
  73.8 1.2 fusion.106
  75.1 1.2 fusion.102
  76.4 1.2 fusion.106
  77.7 1.2 fusion.102
  79.1 1.2 fusion.106
  80.3 1.2 fusion.102
  81.7 1.2 fusion.106
  83.0 5.6 %reduce-scatter.2.cloned.1.call-done = bf16[4,128,896]{2,1,0:T(8,128)(2,1)} async-done(((bf16[16,128,896]{2,1,0:T(8,128)(2,1)}), bf16[4,128,896]{2,1,0:T(8,128)(2,1)}) %reduce-scatter.2.cloned.1.call-update) | async-done | bytes 917520 | tf_op jit(solution)/shard_map/reduce_scatter | solution.py:126
  88.7 21.3 %while.36 = (s32[]{:T(128)}, f32[1,256]{1,0:T(1,128)S(1)}, f32[1,256]{1,0:T(1,128)S(1)}, f32[256,1,128]{0,2,1:T(8,128)S(1)}, bf16[8,512,1,128]{3,1,2,0:T(8,128)(...) while((s32[]{:T(128)}, f32[1,256]{1,0:T(1,128)S(1)}, ...), condition=%wide.region_3.4_spmd.clone, body=%wide.region_0.3_spmd.clone.sunk | while | flops 68782080 | bytes 2192525 | solution.py:83
  88.7 1.2 fusion.95
  90.1 1.2 fusion.99
  91.4 1.2 fusion.95
  92.7 1.2 fusion.99
  94.0 1.2 fusion.95
  95.4 1.2 fusion.99
  96.7 1.2 fusion.95
  98.1 1.2 fusion.99
  99.4 1.2 fusion.95
  100.7 1.2 fusion.99
  102.0 1.2 fusion.95
  103.4 1.2 fusion.99
  104.7 1.2 fusion.95
  106.1 1.2 fusion.99
  107.3 1.2 fusion.95
  108.7 1.2 fusion.99
  110.1 52.5 %all-gather.8.cloned.1.call-done = bf16[16,128,896]{2,1,0:T(8,128)(2,1)} async-done(((bf16[4,128,896]{2,1,0:T(8,128)(2,1)}), bf16[16,128,896]{2,1,0:T(8,128)(2,1)}) %all-gather.8.cloned.1.call-update) | async-done | bytes 3670032 | tf_op jit(solution)/shard_map/all_gather | solution.py:129
  162.6 3.3 %convolution_convert_fusion = bf16[2048,256]{0,1:T(8,128)(2,1)S(1)} fusion(bf16[2048,896]{1,0:T(8,128)(2,1)} %bitcast.160, bf16[112,8,2,128]{3,2,1,0:T(2,128)(2,1)S(1)} %bitcast.162), kind=kOutput, calls=%fused_computation.62 | convolution fusion | flops 940048384 | bytes 5177344 | tf_op jit(solution)/shard_map/dot_general | solution.py:131
  166.1 3.8 %collective-permute-start = (bf16[256,2,1,128]{3,0,1,2:T(8,128)(2,1)S(1)}, bf16[256,2,1,128]{3,0,1,2:T(8,128)(2,1)S(1)}, u32[]{:S(2)}, u32[]{:S(2)}) collective-permute-start(bf16[256,2,1,128]{3,0,1,2:T(8,128)(2,1)S(1)} %copy.39), channel_id=1, source_target_pairs={{0,4},{4,8},{8,12},{12,16},{16,20},{20,24},{24,28},{1,5},{5,9},{9,... | collective-permute-start | bytes 393224 | tf_op jit(solution)/shard_map/ppermute | solution.py:18
  171.0 1.0 copy.40
  173.1 0.7 slice.29
  (134 shorter events, 6.9 us)
Async XLA Ops:
  8.0 28.6 %all-gather.4.cloned.1.call-start = ((), (), s32[]{:S(2)}) async-start(), calls=%async_computation.1 | async-start | bytes 1179648 | tf_op jit(solution)/shard_map/all_gather | solution.py:95
  8.7 53.1 %all-gather.6.cloned.1.call-start = ((), (), s32[]{:S(2)}) async-start(), calls=%async_computation.2 | async-start | bytes 1179648 | tf_op jit(solution)/shard_map/all_gather | solution.py:96
  9.5 79.1 %reduce-scatter.2.cloned.1.call-start = ((), (), s32[]{:S(2)}) async-start(), calls=%async_computation.3 | async-start | bytes 4587520 | tf_op jit(solution)/shard_map/reduce_scatter | solution.py:126
  18.4 0.9 copy-start
  18.4 1.0 copy-start.1
  18.4 144.1 %all-gather.8.cloned.1.call-start = ((), (), s32[]{:S(2)}) async-start(), calls=%async_computation.4 | async-start | bytes 4587520 | tf_op jit(solution)/shard_map/all_gather | solution.py:129
  88.6 73.9 %copy-start.2 = (bf16[896,2,128]{2,1,0:T(2,128)(2,1)S(1)}, bf16[896,2,128]{2,1,0:T(2,128)(2,1)}, u32[]{:S(2)}) copy-start(bf16[896,2,128]{2,1,0:T(2,128)(2,1)} %param.17) | copy-start | bytes 1376260
  166.1 6.0 %collective-permute-start = (bf16[256,2,1,128]{3,0,1,2:T(8,128)(2,1)S(1)}, bf16[256,2,1,128]{3,0,1,2:T(8,128)(2,1)S(1)}, u32[]{:S(2)}, u32[]{:S(2)}) collective-permute-start(bf16[256,2,1,128]{3,0,1,2:T(8,128)(2,1)S(1)} %copy.39), channel_id=1, source_target_pairs={{0,4},{4,8},{8,12},{12,16},{16,20},{20,24},{24,28},{1,5},{5,9},{9,... | collective-permute-start | bytes 393224 | tf_op jit(solution)/shard_map/ppermute | solution.py:18
Sparse Core Ops, SparseCore 0:
  10.7 25.8 all-gather.3
  38.4 23.3 all-gather.5
Sparse Core Ops, SparseCore 1:
  18.5 70.1 reduce-scatter.1
  90.1 72.4 all-gather.7
where the time goes:
time: 183 us; the launch traced here: 181 us
  waiting for transfers between devices  102 us (56%)
  matrix products  47.1 us (26%)
  between operations  15.7 us (9%)
  local copies, waits for them, and re-layouts  6.87 us (4%)
  other arithmetic  4.98 us (3%)
  starting transfers between devices  4.01 us (2%)
    all_gather x1, waiting for transfers between devices, on_device(): joined = lax.all_gather(my_tiles, 'dp', axis=0, tiled=True)  52.5 us
    all_gather x1, waiting for transfers between devices, on_device(): lax.all_gather(values, 'seq', axis=0, tiled=True)  25.3 us
    dot_general x16, matrix products, block_update(): jnp.einsum('hqk,khd->qhd', weights.astype(jnp.bfloat16), value_block, pre...  19.7 us
    dot_general x16, matrix products, block_update(): jnp.einsum('qhd,khd->hqk', query_block, key_block, preferred_element_type...  18.9 us
    all_gather x1, waiting for transfers between devices, on_device(): lax.all_gather(keys, 'seq', axis=0, tiled=True)  16.9 us
    reduce_scatter x1, waiting for transfers between devices, on_device(): lax.psum_scatter(spread_terms.astype(jnp.bfloat16), 'dp', scatter_dimensi...  5.57 us
    dot_general x1, matrix products, on_device(): jnp.einsum('rp,pjn->rjn', chooser, encoded, preferred_element_type=jnp.fl...  4.48 us
    ppermute x1, starting transfers between devices, passed_along(): return lax.ppermute(x, axis, pairs)  3.85 us
  transfers between devices with their start and end apart: 5, of which 4 were waited for; matrix products, arithmetic and copies ran while one was open for 29% of the time, Pallas kernels for 0%

commit v1 on v0

v1 whole, which is shorter than its diff:
```python
import functools
import math

import jax
import jax.numpy as jnp
from jax import lax
from jax.experimental import pallas as pl
from jax.experimental.pallas import tpu as pltpu
from jax.sharding import PartitionSpec as P

HS = 128
NEG = -1e30
MESH = pl.DeviceIdType.MESH


def kernel(
    S, D, tile_len, inv_root,
    ids, q, key, val, cq, enc, w,
    att, crs,
    encv, wall, pbuf, pool, kall, vall, m_ref, l_ref, acc_ref,
    enc_sem, send_w, recv_w, send_p, recv_p, send_x, recv_x, send_s, recv_s,
    send_k, recv_k, send_ks, recv_ks,
):
    C = 2
    G = S // C
    s = lax.axis_index("seq")
    d = lax.axis_index("dp")
    g = s // C
    k = s % C
    sib = g * C + (1 - k)
    T = q.shape[0]
    rows_g = encv.shape[0]
    spans = ids.shape[0]
    span_len = cq.shape[0] // spans

    enc_copy = pltpu.make_async_copy(
        enc.at[pl.ds(pl.multiple_of(g * rows_g, rows_g), rows_g)], encv, enc_sem
    )
    enc_copy.start()

    bar = pltpu.get_barrier_semaphore()

    @pl.loop(1, G)
    def _(o):
        pl.semaphore_signal(bar, 1, device_id={"seq": ((g + o) % G) * C + k}, device_id_type=MESH)

    pl.semaphore_signal(bar, 1, device_id={"seq": sib}, device_id_type=MESH)

    @pl.loop(1, D)
    def _(o):
        pl.semaphore_signal(bar, 1, device_id={"dp": (d + o) % D}, device_id_type=MESH)

    pl.semaphore_wait(bar, G - 1 + 1 + D - 1)

    unit = pool.shape[2]
    units_g = rows_g // unit
    units_tile = tile_len // unit

    def block(plane, group):
        return pl.ds((plane * G + group) * units_g, units_g)

    def w_own(side):
        return pltpu.make_async_remote_copy(
            w.at[k], wall.at[d], send_w.at[side, d], recv_w.at[d],
            device_id={"dp": d + (1 if side else -1)}, device_id_type=MESH)

    def w_pass(src, side):
        return pltpu.make_async_remote_copy(
            wall.at[src], wall.at[src], send_w.at[side, src], recv_w.at[src],
            device_id={"dp": d + (1 if side else -1)}, device_id_type=MESH)

    def p_copy(to, src):
        return pltpu.make_async_remote_copy(
            pbuf.at[to], pool.at[k, block(src, g)], send_p.at[to], recv_p.at[src],
            device_id={"dp": to}, device_id_type=MESH)

    def x_copy(plane, src, to):
        return pltpu.make_async_remote_copy(
            pool.at[k, block(plane, src)], pool.at[k, block(plane, src)],
            send_x.at[plane, to], recv_x.at[plane, src],
            device_id={"seq": to * C + k}, device_id_type=MESH)

    def s_copy(plane, src, kv):
        return pltpu.make_async_remote_copy(
            pool.at[kv, block(plane, src)], pool.at[kv, block(plane, src)],
            send_s.at[plane, src], recv_s.at[plane, src],
            device_id={"seq": sib}, device_id_type=MESH)

    parts = ((0, key, kall), (1, val, vall))

    def kv_copy(i, ref, land, src, to):
        return pltpu.make_async_remote_copy(
            ref, land.at[src * C + k], send_k.at[i, to], recv_k.at[i, src],
            device_id={"seq": to * C + k}, device_id_type=MESH)

    def kv_sib(i, src_ref, land, src, kk):
        return pltpu.make_async_remote_copy(
            src_ref, land.at[src * C + kk], send_ks.at[i, src], recv_ks.at[i, src],
            device_id={"seq": sib}, device_id_type=MESH)

    for side in (0, 1):
        @pl.when((d + 1 < D) if side else (d > 0))
        def _():
            w_own(side).start()

    @pl.loop(g + 1, G)
    def _(to):
        for i, ref, land in parts:
            kv_copy(i, ref, land, g, to).start()

    @pl.when(k == 0)
    def _():
        for i, ref, land in parts:
            kv_sib(i, ref, land, g, 0).start()

    def project(weight):
        return jnp.dot(encv[...], weight, preferred_element_type=jnp.float32).astype(jnp.bfloat16)

    def spread(plane):
        @pl.loop(1, G)
        def _(o):
            x_copy(plane, g, (g + o) % G).start()

        s_copy(plane, g, k).start()

    enc_copy.wait()
    pool[k, block(d, g)] = project(w[k]).reshape(units_g, unit, HS)
    spread(d)

    @pl.loop(1, D)
    def _(e):
        for side in (1, 0):
            src = d - e if side else d + e

            @pl.when((src >= 0) if side else (src < D))
            def _():
                w_pass(src, side).wait_recv()

                @pl.when((d + 1 < D) if side else (d > 0))
                def _():
                    w_pass(src, side).start()

                pbuf[src] = project(wall[src]).reshape(units_g, unit, HS)
                p_copy(src, d).start()

    half = T // 2

    def own_part(h):
        rows = pl.ds(h * half, half)
        sc = lax.dot_general(q[rows, :], key[...], (((1,), (1,)), ((), ())),
                             preferred_element_type=jnp.float32) * inv_root
        r = lax.broadcasted_iota(jnp.int32, sc.shape, 0) + h * half
        c = lax.broadcasted_iota(jnp.int32, sc.shape, 1)
        sc = jnp.where(c <= r, sc, NEG)
        mx = jnp.max(sc, axis=1, keepdims=True)
        ex = jnp.where(c <= r, jnp.exp(sc - mx), 0.0)
        m_ref[rows, :] = mx
        l_ref[rows, :] = jnp.sum(ex, axis=1, keepdims=True)
        acc_ref[rows, :] = jnp.dot(ex.astype(jnp.bfloat16), val[...],
                                   preferred_element_type=jnp.float32)

    for h in range(2):
        own_part(h)

    @pl.loop(0, g)
    def _(src):
        for i, ref, land in parts:
            kv_copy(i, ref, land, src, g).wait_recv()
            kv_sib(i, land.at[src * C + k], land, src, k).start()

    @pl.loop(1, D)
    def _(e):
        for side in (1, 0):
            src = d - e if side else d + e

            @pl.when((src >= 0) if side else (src < D))
            def _():
                p_copy(d, src).wait_recv()
                spread(src)

    @pl.loop(0, g)
    def _(src):
        for i, ref, land in parts:
            kv_sib(i, ref, land, src, 1 - k).wait_recv()

    @pl.when(k == 1)
    def _():
        for i, ref, land in parts:
            kv_sib(i, ref, land, g, 0).wait_recv()

    @pl.loop(0, s)
    def _(b):
        for h in range(2):
            rows = pl.ds(h * half, half)
            sc = lax.dot_general(q[rows, :], kall[b], (((1,), (1,)), ((), ())),
                                 preferred_element_type=jnp.float32) * inv_root
            old = m_ref[rows, :]
            mx = jnp.maximum(old, jnp.max(sc, axis=1, keepdims=True))
            ex = jnp.exp(sc - mx)
            fade = jnp.exp(old - mx)
            m_ref[rows, :] = mx
            l_ref[rows, :] = l_ref[rows, :] * fade + jnp.sum(ex, axis=1, keepdims=True)
            acc_ref[rows, :] = acc_ref[rows, :] * fade + jnp.dot(
                ex.astype(jnp.bfloat16), vall[b], preferred_element_type=jnp.float32)

    att[...] = (acc_ref[...] / l_ref[...]).astype(jnp.bfloat16)

    def pass_plane(plane):
        @pl.loop(1, G)
        def _(o):
            src = (g + o) % G
            x_copy(plane, src, g).wait_recv()
            s_copy(plane, src, k).start()

    pass_plane(d)

    @pl.loop(1, D)
    def _(e):
        for side in (1, 0):
            src = d - e if side else d + e

            @pl.when((src >= 0) if side else (src < D))
            def _():
                pass_plane(src)

    @pl.loop(0, D)
    def _(plane):
        @pl.loop(0, G)
        def _(src):
            s_copy(plane, src, 1 - k).wait_recv()

    for b in range(spans):
        ck, cv = (
            jnp.concatenate([pool[kv, ids[b, n] * units_tile + u]
                             for n in range(ids.shape[1]) for u in range(units_tile)], axis=0)
            for kv in range(2)
        )
        sc = lax.dot_general(cq[b * span_len:(b + 1) * span_len, :], ck, (((1,), (1,)), ((), ())),
                             preferred_element_type=jnp.float32) * inv_root
        mx = jnp.max(sc, axis=1, keepdims=True)
        ex = jnp.exp(sc - mx)
        tot = jnp.sum(ex, axis=1, keepdims=True)
        out = jnp.dot(ex.astype(jnp.bfloat16), cv, preferred_element_type=jnp.float32) / tot
        if b == 0:
            out = jnp.where(s > 0, out, 0.0)
        crs[b * span_len:(b + 1) * span_len, :] = out.astype(jnp.bfloat16)

    for side in (0, 1):
        @pl.when((d + 1 < D) if side else (d > 0))
        def _():
            w_own(side).wait_send()

            @pl.loop(0, D)
            def _(src):
                @pl.when((src < d) if side else (src > d))
                def _():
                    w_pass(src, side).wait_send()

    @pl.loop(1, D)
    def _(o):
        p_copy((d + o) % D, d).wait_send()

    @pl.loop(0, D)
    def _(plane):
        @pl.loop(1, G)
        def _(o):
            x_copy(plane, g, (g + o) % G).wait_send()

        @pl.loop(0, G)
        def _(src):
            s_copy(plane, src, k).wait_send()

    @pl.loop(g + 1, G)
    def _(to):
        for i, ref, land in parts:
            kv_copy(i, ref, land, g, to).wait_send()

    @pl.when(k == 0)
    def _():
        for i, ref, land in parts:
            kv_sib(i, ref, land, g, 0).wait_send()

    @pl.loop(0, g)
    def _(src):
        for i, ref, land in parts:
            kv_sib(i, land.at[src * C + k], land, src, k).wait_send()


def on_device(queries, keys, values, cross_queries, encoded, cross_kv_weight, owners, tile_rows):
    S, D = lax.axis_size("seq"), lax.axis_size("dp")
    G = S // 2
    T, width = queries.shape
    pool_here, tile_len, wide = encoded.shape
    rows_here = pool_here * tile_len
    rows_g = rows_here // G
    unit = math.gcd(rows_g, tile_len)
    spans_here = owners.shape[0]
    span_len = T // spans_here
    tile_index = owners * pool_here + tile_rows
    before = lax.ppermute(tile_index[-1:], "seq", [(i, i + 1) for i in range(S - 1)])
    ids = jnp.concatenate([before, tile_index], axis=0)
    padded = jnp.pad(cross_queries, ((1, span_len - 1), (0, 0)))
    w = jnp.transpose(cross_kv_weight, (1, 0, 2))
    bf, f32 = jnp.bfloat16, jnp.float32
    vm = pl.BlockSpec(memory_space=pltpu.VMEM)
    dma = pltpu.SemaphoreType.DMA
    attended, crossed = pl.pallas_call(
        functools.partial(kernel, S, D, tile_len, 1.0 / math.sqrt(HS)),
        name="retro",
        out_shape=(jax.ShapeDtypeStruct((T, width), bf), jax.ShapeDtypeStruct(padded.shape, bf)),
        in_specs=[pl.BlockSpec(memory_space=pltpu.SMEM), vm, vm, vm, vm,
                  pl.BlockSpec(memory_space=pl.ANY), vm],
        out_specs=(vm, vm),
        scratch_shapes=[
            pltpu.VMEM((rows_g, wide), bf),
            pltpu.VMEM((D, wide, HS), bf),
            pltpu.VMEM((D, rows_g // unit, unit, HS), bf),
            pltpu.VMEM((2, D * rows_here // unit, unit, HS), bf),
            pltpu.VMEM((S, T, HS), bf),
            pltpu.VMEM((S, T, HS), bf),
            pltpu.VMEM((T, 1), f32),
            pltpu.VMEM((T, 1), f32),
            pltpu.VMEM((T, HS), f32),
            dma, dma((2, D)), dma((D,)), dma((D,)), dma((D,)),
            dma((D, G)), dma((D, G)), dma((D, G)), dma((D, G)),
            dma((2, G)), dma((2, G)), dma((2, G)), dma((2, G)),
        ],
        compiler_params=pltpu.CompilerParams(
            collective_id=0, has_side_effects=True, vmem_limit_bytes=60 * 1024 * 1024),
    )(ids, queries, keys, values, padded, encoded.reshape(rows_here, wide), w)
    return attended, crossed[1:T + 1]


def solution(mesh):
    placed = (
        P("seq", "dp"),
        P("seq", "dp"),
        P("seq", "dp"),
        P("seq", "dp"),
        P("dp", None, None),
        P(None, None, "dp"),
        P("seq", None),
        P("seq", None),
    )
    return jax.shard_map(
        on_device,
        mesh=mesh,
        in_specs=placed,
        out_specs=(P("seq", "dp"), P("seq", "dp")),
        check_vma=False,
    )
```

time: 183 us -> 74.6 us (0.41)
  waiting for transfers between devices: 102 us -> 0.01 us
  Pallas kernels: 0 us -> 61 us
  matrix products: 47.1 us -> 0 us
  between operations: 15.7 us -> 0.65 us
  other arithmetic: 4.98 us -> 0.78 us
    all_gather x3 -> x0, waiting for transfers between devices: 94.7 us -> none  [the longest x1 52.5 us: on_device(): joined = lax.all_gather(my_tiles, 'dp', axis=0, tiled=True)]
    pallas_call x0 -> x1, Pallas kernels: none -> 61 us  [on_device(): pl.pallas_call(functools.partial(kernel, S, D, tile_len, 1.0 / math.sqrt(...]
    dot_general x36 -> x0, matrix products: 47.1 us -> none  [the longest x16 19.7 us: block_update(): jnp.einsum('hqk,khd->qhd', weights.astype(jnp.bfloat16), value_block, pre...]
    reduce_scatter x1 -> x0, waiting for transfers between devices: 5.57 us -> none  [on_device(): lax.psum_scatter(spread_terms.astype(jnp.bfloat16), 'dp', scatter_dimensi...]
    reduce_sum x17 -> x0, other arithmetic: 2.72 us -> none  [the longest x16 2.43 us: block_update(): new_total = running_total * fading + jnp.sum(weights, axis=2)]
    convert_element_type x1 -> x0, local copies, waits for them, and re-layouts: 2.64 us -> none  [on_device(): spread_terms.astype(jnp.bfloat16)]
  transfers between devices with their start and end apart: 5 -> 1, of which waited for: 4 -> 0; matrix products, arithmetic and copies ran while one was open for 29% -> 5% of each run, Pallas kernels for 0% -> 0%
where the time goes in v1:
time: 74.6 us; the launch traced here: 74.3 us
  Pallas kernels  61 us (82%)
  local copies, waits for them, and re-layouts  7.37 us (10%)
  starting transfers between devices  4.49 us (6%)
  other arithmetic  0.78 us (1%)
    pallas_call x1, Pallas kernels, on_device(): pl.pallas_call(functools.partial(kernel, S, D, tile_len, 1.0 / math.sqrt(...  61 us
    ppermute x1, starting transfers between devices, on_device(): lax.ppermute(tile_index[-1:], 'seq', [(i, i + 1) for i in range(S - 1)])  4.49 us
    unnamed x2, local copies, waits for them, and re-layouts  3.41 us
    pad x1, local copies, waits for them, and re-layouts, on_device(): padded = jnp.pad(cross_queries, ((1, span_len - 1), (0, 0)))  1.6 us
    slice x1, local copies, waits for them, and re-layouts, on_device(): return (attended, crossed[1:T + 1])  1.6 us
  transfers between devices with their start and end apart: 1, of which 0 were waited for; matrix products, arithmetic and copies ran while one was open for 5% of the time, Pallas kernels for 0%

profile of v1, /device:TPU:1, one launch (start us, length us, event | category | flops | bytes accessed | tf_op | source)
XLA Modules:
  0.0 74.3 jit_solution(17666007934358334468)
XLA Ops:
  0.6 0.7 multiply_add_fusion
  1.3 0.1 slice.6
  1.4 4.5 %collective-permute-start = (s32[1,2]{0,1:T(2,128)S(1)}, s32[1,2]{0,1:T(2,128)S(1)}, u32[]{:S(2)}, u32[]{:S(2)}) collective-permute-start(s32[1,2]{0,1:T(2,128)S(1)} %slice.6), channel_id=1, source_target_pairs={{0,4},{4,8},{8,12},{12,16},{16,20},{20,24},{24,28},{1,5},{5,9},{9,... | collective-permute-start | bytes 32 | tf_op jit(solution)/shard_map/ppermute | solution.py:300
  5.9 1.8 %copy.16 = bf16[896,2,128]{2,0,1:T(8,128)(2,1)} copy(bf16[896,2,128]{2,1,0:T(2,128)(2,1)} %param.13) | data formatting | bytes 917504 | tf_op args[5]
  7.7 1.6 %pad.4.cq = bf16[576,128]{1,0:T(8,128)(2,1)} pad(bf16[512,128]{1,0:T(8,128)(2,1)} %param.11, bf16[]{:T(256)} %constant.4.clone.1), padding=1_63x0_0 | pad | bytes 278530 | tf_op jit(solution)/shard_map/jit(_pad)/pad | solution.py:302
  9.4 0.0 collective-permute-done
  9.4 0.1 pad_add_fusion
  9.4 0.7 copy.14.ids
  10.1 61.0 %retro.1 = (bf16[512,128]{1,0:T(8,128)(2,1)}, bf16[576,128]{1,0:T(8,128)(2,1)}) custom-call(s32[9,2]{1,0:T(8,128)} %copy.14.ids, bf16[512,128]{1,0:T(8,128)(2,1)} %q.1, bf16[512,128]{1,0:T(8,128)(2,1)} %key.1, bf16[512,128]{1,0:T(8,128)(2,1)} %val.1, bf16[576,128]{1,0:T(8,128)(2,1)} %pad.4.cq, bf16[2048,896]{1,0:T(8,128)(2,1)} %bitcast.4, ...), custom_call_target="tpu_custom_call" | custom-call | tf_op jit(solution)/shard_map/retro/pallas_call | solution.py:307
  71.1 1.6 %slice.7 = bf16[512,128]{1,0:T(8,128)(2,1)} slice(bf16[576,128]{1,0:T(8,128)(2,1)} %get-tuple-element.5), slice={[1:513], [0:128]} | slice | bytes 262144 | tf_op jit(solution)/shard_map/slice | solution.py:331
  72.7 1.6 %copy.18 = bf16[512,128]{1,0:T(8,128)(2,1)} copy(bf16[512,128]{1,0:T(8,128)(2,1)} %get-tuple-element.8) | data formatting | bytes 262144
Async XLA Ops:
  1.4 7.9 %collective-permute-start = (s32[1,2]{0,1:T(2,128)S(1)}, s32[1,2]{0,1:T(2,128)S(1)}, u32[]{:S(2)}, u32[]{:S(2)}) collective-permute-start(s32[1,2]{0,1:T(2,128)S(1)} %slice.6), channel_id=1, source_target_pairs={{0,4},{4,8},{8,12},{12,16},{16,20},{20,24},{24,28},{1,5},{5,9},{9,... | collective-permute-start | bytes 32 | tf_op jit(solution)/shard_map/ppermute | solution.py:300

commit v2 on v1

--- a/solution.py
+++ b/solution.py
@@ -15,10 +15,10 @@
 
 def kernel(
     S, D, tile_len, inv_root,
-    ids, q, key, val, cq, enc, w,
+    own_s, row_s, own_h, row_h, q, key, val, cq, enc, w,
     att, crs,
-    encv, wall, pbuf, pool, kall, vall, m_ref, l_ref, acc_ref,
-    enc_sem, send_w, recv_w, send_p, recv_p, send_x, recv_x, send_s, recv_s,
+    prev_v, prev_s, cqp, crf, encv, wall, pbuf, pool, kall, vall, m_ref, l_ref, acc_ref,
+    enc_sem, id_send, id_recv, id_sem, send_w, recv_w, send_p, recv_p, send_x, recv_x, send_s, recv_s,
     send_k, recv_k, send_ks, recv_ks,
 ):
     C = 2
@@ -30,8 +30,10 @@
     sib = g * C + (1 - k)
     T = q.shape[0]
     rows_g = encv.shape[0]
-    spans = ids.shape[0]
-    span_len = cq.shape[0] // spans
+    near, spans_here = own_s.shape
+    spans = spans_here + 1
+    span_len = T // spans_here
+    pool_here = (encv.shape[0] * G) // tile_len
 
     enc_copy = pltpu.make_async_copy(
         enc.at[pl.ds(pl.multiple_of(g * rows_g, rows_g), rows_g)], encv, enc_sem
@@ -50,7 +52,23 @@
     def _(o):
         pl.semaphore_signal(bar, 1, device_id={"dp": (d + o) % D}, device_id_type=MESH)
 
-    pl.semaphore_wait(bar, G - 1 + 1 + D - 1)
+    nxt = (s + 1) % S
+    prv = (s + S - 1) % S
+
+    @pl.when(k == 1)
+    def _():
+        pl.semaphore_signal(bar, 1, device_id={"seq": nxt}, device_id_type=MESH)
+
+    @pl.when(k == 0)
+    def _():
+        pl.semaphore_signal(bar, 1, device_id={"seq": prv}, device_id_type=MESH)
+
+    pl.semaphore_wait(bar, G - 1 + 1 + D - 1 + 1)
+
+    def id_copy(i, ref):
+        return pltpu.make_async_remote_copy(
+            ref, prev_v.at[i], id_send.at[i], id_recv.at[i],
+            device_id={"seq": nxt}, device_id_type=MESH)
 
     unit = pool.shape[2]
     units_g = rows_g // unit
@@ -103,6 +121,9 @@
         def _():
             w_own(side).start()
 
+    for i, ref in ((0, own_h), (1, row_h)):
+        id_copy(i, ref).start()
+
     @pl.loop(g + 1, G)
     def _(to):
         for i, ref, land in parts:
@@ -127,23 +148,9 @@
     pool[k, block(d, g)] = project(w[k]).reshape(units_g, unit, HS)
     spread(d)
 
-    @pl.loop(1, D)
-    def _(e):
-        for side in (1, 0):
-            src = d - e if side else d + e
-
-            @pl.when((src >= 0) if side else (src < D))
-            def _():
-                w_pass(src, side).wait_recv()
-
-                @pl.when((d + 1 < D) if side else (d > 0))
-                def _():
-                    w_pass(src, side).start()
-
-                pbuf[src] = project(wall[src]).reshape(units_g, unit, HS)
-                p_copy(src, d).start()
-
-    half = T // 2
+    shifted = jnp.concatenate(
+        [cq[...].astype(jnp.float32), jnp.zeros((span_len, HS), jnp.float32)], axis=0)
+    cqp[...] = pltpu.roll(shifted, 1, 0).astype(jnp.bfloat16)
 
     def own_part(h):
         rows = pl.ds(h * half, half)
@@ -159,24 +166,50 @@
         acc_ref[rows, :] = jnp.dot(ex.astype(jnp.bfloat16), val[...],
                                    preferred_element_type=jnp.float32)
 
+    half = T // 2
     for h in range(2):
         own_part(h)
 
-    @pl.loop(0, g)
-    def _(src):
-        for i, ref, land in parts:
-            kv_copy(i, ref, land, src, g).wait_recv()
-            kv_sib(i, land.at[src * C + k], land, src, k).start()
-
-    @pl.loop(1, D)
+    @pl.loop(1, D + 1)
     def _(e):
-        for side in (1, 0):
-            src = d - e if side else d + e
-
-            @pl.when((src >= 0) if side else (src < D))
-            def _():
-                p_copy(d, src).wait_recv()
-                spread(src)
+        @pl.when(e < D)
+        def _():
+            for side in (1, 0):
+                src = d - e if side else d + e
+
+                @pl.when((src >= 0) if side else (src < D))
+                def _():
+                    w_pass(src, side).wait_recv()
+
+                    @pl.when((d + 1 < D) if side else (d > 0))
+                    def _():
+                        w_pass(src, side).start()
+
+            for side in (1, 0):
+                src = d - e if side else d + e
+
+                @pl.when((src >= 0) if side else (src < D))
+                def _():
+                    pbuf[src] = project(wall[src]).reshape(units_g, unit, HS)
+                    p_copy(src, d).start()
+
+        @pl.when(e == D - 1)
+        def _():
+            @pl.loop(0, g)
+            def _(src):
+                for i, ref, land in parts:
+                    kv_copy(i, ref, land, src, g).wait_recv()
+                    kv_sib(i, land.at[src * C + k], land, src, k).start()
+
+        @pl.when(e > 1)
+        def _():
+            for side in (1, 0):
+                src = d - (e - 1) if side else d + (e - 1)
+
+                @pl.when((src >= 0) if side else (src < D))
+                def _():
+                    p_copy(d, src).wait_recv()
+                    spread(src)
 
     @pl.loop(0, g)
     def _(src):
@@ -229,13 +262,24 @@
         def _(src):
             s_copy(plane, src, 1 - k).wait_recv()
 
+    for i, ref in ((0, own_h), (1, row_h)):
+        id_copy(i, ref).wait_recv()
+        pltpu.make_async_copy(prev_v.at[i], prev_s.at[i], id_sem.at[i]).start()
+    for i in range(2):
+        pltpu.make_async_copy(prev_v.at[i], prev_s.at[i], id_sem.at[i]).wait()
     for b in range(spans):
+        tiles = []
+        for n in range(near):
+            if b == 0:
+                tiles.append(prev_s[0, n, spans_here - 1] * pool_here + prev_s[1, n, spans_here - 1])
+            else:
+                tiles.append(own_s[n, b - 1] * pool_here + row_s[n, b - 1])
         ck, cv = (
-            jnp.concatenate([pool[kv, ids[b, n] * units_tile + u]
-                             for n in range(ids.shape[1]) for u in range(units_tile)], axis=0)
+            jnp.concatenate([pool[kv, tile * units_tile + u]
+                             for tile in tiles for u in range(units_tile)], axis=0)
             for kv in range(2)
         )
-        sc = lax.dot_general(cq[b * span_len:(b + 1) * span_len, :], ck, (((1,), (1,)), ((), ())),
+        sc = lax.dot_general(cqp[b * span_len:(b + 1) * span_len, :], ck, (((1,), (1,)), ((), ())),
                              preferred_element_type=jnp.float32) * inv_root
         mx = jnp.max(sc, axis=1, keepdims=True)
         ex = jnp.exp(sc - mx)
@@ -243,7 +287,12 @@
         out = jnp.dot(ex.astype(jnp.bfloat16), cv, preferred_element_type=jnp.float32) / tot
         if b == 0:
             out = jnp.where(s > 0, out, 0.0)
-        crs[b * span_len:(b + 1) * span_len, :] = out.astype(jnp.bfloat16)
+        crf[b * span_len:(b + 1) * span_len, :] = out
+    back = pltpu.roll(crf[...], T + span_len - 1, 0)
+    crs[...] = back[:T].astype(jnp.bfloat16)
+
+    for i, ref in ((0, own_h), (1, row_h)):
+        id_copy(i, ref).wait_send()
 
     for side in (0, 1):
         @pl.when((d + 1 < D) if side else (d > 0))
@@ -296,22 +345,26 @@
     unit = math.gcd(rows_g, tile_len)
     spans_here = owners.shape[0]
     span_len = T // spans_here
-    tile_index = owners * pool_here + tile_rows
-    before = lax.ppermute(tile_index[-1:], "seq", [(i, i + 1) for i in range(S - 1)])
-    ids = jnp.concatenate([before, tile_index], axis=0)
-    padded = jnp.pad(cross_queries, ((1, span_len - 1), (0, 0)))
     w = jnp.transpose(cross_kv_weight, (1, 0, 2))
+    own, row = owners.T, tile_rows.T
+    near = own.shape[0]
     bf, f32 = jnp.bfloat16, jnp.float32
     vm = pl.BlockSpec(memory_space=pltpu.VMEM)
     dma = pltpu.SemaphoreType.DMA
     attended, crossed = pl.pallas_call(
         functools.partial(kernel, S, D, tile_len, 1.0 / math.sqrt(HS)),
         name="retro",
-        out_shape=(jax.ShapeDtypeStruct((T, width), bf), jax.ShapeDtypeStruct(padded.shape, bf)),
-        in_specs=[pl.BlockSpec(memory_space=pltpu.SMEM), vm, vm, vm, vm,
+        out_shape=(jax.ShapeDtypeStruct((T, width), bf), jax.ShapeDtypeStruct((T, width), bf)),
+        in_specs=[pl.BlockSpec(memory_space=pltpu.SMEM)] * 2
+                 + [pl.BlockSpec(memory_space=pl.ANY)] * 2
+                 + [vm, vm, vm, vm,
                   pl.BlockSpec(memory_space=pl.ANY), vm],
         out_specs=(vm, vm),
         scratch_shapes=[
+            pltpu.VMEM((2, near, spans_here), jnp.int32),
+            pltpu.SMEM((2, near, spans_here), jnp.int32),
+            pltpu.VMEM((T + span_len, HS), bf),
+            pltpu.VMEM((T + span_len, HS), f32),
             pltpu.VMEM((rows_g, wide), bf),
             pltpu.VMEM((D, wide, HS), bf),
             pltpu.VMEM((D, rows_g // unit, unit, HS), bf),
@@ -321,14 +374,14 @@
             pltpu.VMEM((T, 1), f32),
             pltpu.VMEM((T, 1), f32),
             pltpu.VMEM((T, HS), f32),
-            dma, dma((2, D)), dma((D,)), dma((D,)), dma((D,)),
+            dma, dma((2,)), dma((2,)), dma((2,)), dma((2, D)), dma((D,)), dma((D,)), dma((D,)),
             dma((D, G)), dma((D, G)), dma((D, G)), dma((D, G)),
             dma((2, G)), dma((2, G)), dma((2, G)), dma((2, G)),
         ],
         compiler_params=pltpu.CompilerParams(
             collective_id=0, has_side_effects=True, vmem_limit_bytes=60 * 1024 * 1024),
-    )(ids, queries, keys, values, padded, encoded.reshape(rows_here, wide), w)
-    return attended, crossed[1:T + 1]
+    )(own, row, own, row, queries, keys, values, cross_queries, encoded.reshape(rows_here, wide), w)
+    return attended, crossed
 
 
 def solution(mesh):

time: 74.6 us -> 53.4 us (0.72)
  Pallas kernels: 61 us -> 47.5 us
  starting transfers between devices: 4.49 us -> 0 us
  local copies, waits for them, and re-layouts: 7.37 us -> 4.98 us
  other arithmetic: 0.78 us -> 0 us
    pallas_call x1, Pallas kernels: 61 us -> 47.5 us  [on_device(): pl.pallas_call(functools.partial(kernel, S, D, tile_len, 1.0 / math.sqrt(...]
    ppermute x1 -> x0, starting transfers between devices: 4.49 us -> none  [on_device(): lax.ppermute(tile_index[-1:], 'seq', [(i, i + 1) for i in range(S - 1)])]
    slice x2 -> x0, local copies, waits for them, and re-layouts: 1.67 us -> none  [the longest x1 1.6 us: on_device(): return (attended, crossed[1:T + 1])]
    pad x1 -> x0, local copies, waits for them, and re-layouts: 1.6 us -> none  [on_device(): padded = jnp.pad(cross_queries, ((1, span_len - 1), (0, 0)))]
    unnamed x2 -> x3, local copies, waits for them, and re-layouts: 3.41 us -> 4.98 us
  transfers between devices with their start and end apart: 1 -> 0, of which waited for: 0 -> 0; matrix products, arithmetic and copies ran while one was open for 5% -> 0% of each run, Pallas kernels for 0% -> 0%
where the time goes in v2:
time: 53.4 us; the launch traced here: 53.1 us
  Pallas kernels  47.5 us (89%)
  local copies, waits for them, and re-layouts  4.98 us (9%)
  between operations  0.64 us (1%)
    pallas_call x1, Pallas kernels, on_device(): pl.pallas_call(functools.partial(kernel, S, D, tile_len, 1.0 / math.sqrt(...  47.5 us
    unnamed x3, local copies, waits for them, and re-layouts  4.98 us

profile of v2, /device:TPU:1, one launch (start us, length us, event | category | flops | bytes accessed | tf_op | source)
XLA Modules:
  0.0 53.1 jit_solution(3082384948149279640)
XLA Ops:
  0.6 1.8 %copy.12 = bf16[896,2,128]{2,0,1:T(8,128)(2,1)} copy(bf16[896,2,128]{2,1,0:T(2,128)(2,1)} %param.13) | data formatting | bytes 917504 | tf_op args[5]
  2.5 47.5 %retro.1 = (bf16[512,128]{1,0:T(8,128)(2,1)}, bf16[512,128]{1,0:T(8,128)(2,1)}) custom-call(s32[2,8]{1,0:T(2,128)} %bitcast.8, s32[2,8]{1,0:T(2,128)} %bitcast.10, s32[2,8]{1,0:T(2,128)} %bitcast.9, s32[2,8]{1,0:T(2,128)} %bitcast.11, bf16[512,128]{1,0:T(8,128)(2,1)} %q.1, bf16[512,128]{1,0:T(8,128)(2,1)} %key.1, bf16[512,128]{1,0:T(8,128)(2,1)} %val.1, ...), custom_call_target="tpu_custom_call" | custom-call | tf_op jit(solution)/shard_map/retro/pallas_call | solution.py:354
  50.0 1.6 %copy.15 = bf16[512,128]{1,0:T(8,128)(2,1)} copy(bf16[512,128]{1,0:T(8,128)(2,1)} %get-tuple-element.4) | data formatting | bytes 262144
  51.5 1.6 %copy.16 = bf16[512,128]{1,0:T(8,128)(2,1)} copy(bf16[512,128]{1,0:T(8,128)(2,1)} %get-tuple-element.5) | data formatting | bytes 262144

commit v3 on v2

--- a/solution.py
+++ b/solution.py
@@ -18,7 +18,7 @@
     own_s, row_s, own_h, row_h, q, key, val, cq, enc, w,
     att, crs,
     prev_v, prev_s, cqp, crf, encv, wall, pbuf, pool, kall, vall, m_ref, l_ref, acc_ref,
-    enc_sem, id_send, id_recv, id_sem, send_w, recv_w, send_p, recv_p, send_x, recv_x, send_s, recv_s,
+    enc_sem, id_send, id_recv, id_sem, send_w, recv_w, send_p, recv_p, send_x, send_f, recv_x, send_s, recv_s,
     send_k, recv_k, send_ks, recv_ks,
 ):
     C = 2
@@ -92,11 +92,33 @@
             pbuf.at[to], pool.at[k, block(src, g)], send_p.at[to], recv_p.at[src],
             device_id={"dp": to}, device_id_type=MESH)
 
-    def x_copy(plane, src, to):
-        return pltpu.make_async_remote_copy(
-            pool.at[k, block(plane, src)], pool.at[k, block(plane, src)],
-            send_x.at[plane, to], recv_x.at[plane, src],
+    wide_x = 2 if G % 2 == 0 else 1
+    high = G // wide_x
+    gy, gx = g // wide_x, g % wide_x
+    has_x = wide_x == 2
+    gxn = gy * wide_x + (1 - gx) if has_x else g
+    half_u = units_g // 2
+
+    def up(o):
+        return ((gy + o) % high) * wide_x + gx
+
+    def x_copy(plane, src, h, to, sem):
+        part = pl.ds((plane * G + src) * units_g + h * half_u, half_u)
+        return pltpu.make_async_remote_copy(
+            pool.at[k, part], pool.at[k, part], sem, recv_x.at[plane, h, src],
             device_id={"seq": to * C + k}, device_id_type=MESH)
+
+    def x_own(plane, h, to):
+        return x_copy(plane, g, h, to, send_x.at[plane, h, to])
+
+    def x_fwd0(plane, to):
+        return x_copy(plane, gxn, 0, to, send_f.at[plane, 0, to])
+
+    def x_fwd1(plane, src):
+        return x_copy(plane, src, 1, gxn, send_f.at[plane, 1, src])
+
+    def x_wait(plane, src, h):
+        x_copy(plane, src, h, g, recv_x.at[plane, h, src]).wait_recv()
 
     def s_copy(plane, src, kv):
         return pltpu.make_async_remote_copy(
@@ -138,11 +160,65 @@
         return jnp.dot(encv[...], weight, preferred_element_type=jnp.float32).astype(jnp.bfloat16)
 
     def spread(plane):
-        @pl.loop(1, G)
-        def _(o):
-            x_copy(plane, g, (g + o) % G).start()
+        if has_x:
+            x_own(plane, 0, gxn).start()
+
+        @pl.loop(1, high)
+        def _(o):
+            x_own(plane, 1, up(o)).start()
+
+        if has_x:
+            x_own(plane, 1, gxn).start()
+
+        @pl.loop(1, high)
+        def _(o):
+            x_own(plane, 0, up(o)).start()
 
         s_copy(plane, g, k).start()
+
+    def relay(plane):
+        if has_x:
+            x_wait(plane, gxn, 0)
+
+        @pl.loop(1, high)
+        def _(o):
+            if has_x:
+                x_fwd0(plane, up(o)).start()
+            x_wait(plane, up(o), 1)
+            if has_x:
+                x_fwd1(plane, up(o)).start()
+
+        if has_x:
+            x_wait(plane, gxn, 1)
+            s_copy(plane, gxn, k).start()
+
+        @pl.loop(1, high)
+        def _(o):
+            x_wait(plane, up(o), 0)
+            s_copy(plane, up(o), k).start()
+
+    def finish(plane):
+        @pl.loop(1, high)
+        def _(o):
+            if has_x:
+                far = ((gy + o) % high) * wide_x + (1 - gx)
+                x_wait(plane, far, 0)
+                x_wait(plane, far, 1)
+                s_copy(plane, far, k).start()
+
+    def at_distance(e, what):
+        @pl.when(e == 0)
+        def _():
+            what(d)
+
+        @pl.when(e > 0)
+        def _():
+            for side in (1, 0):
+                src = d - e if side else d + e
+
+                @pl.when((src >= 0) if side else (src < D))
+                def _():
+                    what(src)
 
     enc_copy.wait()
     pool[k, block(d, g)] = project(w[k]).reshape(units_g, unit, HS)
@@ -170,7 +246,37 @@
     for h in range(2):
         own_part(h)
 
-    @pl.loop(1, D + 1)
+    chunks = 3
+
+    def earlier_keys(chunk):
+        @pl.when(chunk == 0)
+        def _():
+            @pl.loop(0, g)
+            def _(src):
+                for i, ref, land in parts:
+                    kv_sib(i, ref, land, src, 1 - k).wait_recv()
+
+            @pl.when(k == 1)
+            def _():
+                for i, ref, land in parts:
+                    kv_sib(i, ref, land, g, 0).wait_recv()
+
+        @pl.loop(chunk * s // chunks, (chunk + 1) * s // chunks)
+        def _(b):
+            for h in range(2):
+                rows = pl.ds(h * half, half)
+                sc = lax.dot_general(q[rows, :], kall[b], (((1,), (1,)), ((), ())),
+                                     preferred_element_type=jnp.float32) * inv_root
+                old = m_ref[rows, :]
+                mx = jnp.maximum(old, jnp.max(sc, axis=1, keepdims=True))
+                ex = jnp.exp(sc - mx)
+                fade = jnp.exp(old - mx)
+                m_ref[rows, :] = mx
+                l_ref[rows, :] = l_ref[rows, :] * fade + jnp.sum(ex, axis=1, keepdims=True)
+                acc_ref[rows, :] = acc_ref[rows, :] * fade + jnp.dot(
+                    ex.astype(jnp.bfloat16), vall[b], preferred_element_type=jnp.float32)
+
+    @pl.loop(1, D + 2)
     def _(e):
         @pl.when(e < D)
         def _():
@@ -201,60 +307,27 @@
                     kv_copy(i, ref, land, src, g).wait_recv()
                     kv_sib(i, land.at[src * C + k], land, src, k).start()
 
+        @pl.when((e > 1) & (e <= D))
+        def _():
+            def arrive(src):
+                p_copy(d, src).wait_recv()
+                spread(src)
+
+            at_distance(e - 1, arrive)
+
         @pl.when(e > 1)
         def _():
-            for side in (1, 0):
-                src = d - (e - 1) if side else d + (e - 1)
-
-                @pl.when((src >= 0) if side else (src < D))
-                def _():
-                    p_copy(d, src).wait_recv()
-                    spread(src)
-
-    @pl.loop(0, g)
-    def _(src):
-        for i, ref, land in parts:
-            kv_sib(i, ref, land, src, 1 - k).wait_recv()
-
-    @pl.when(k == 1)
-    def _():
-        for i, ref, land in parts:
-            kv_sib(i, ref, land, g, 0).wait_recv()
-
-    @pl.loop(0, s)
-    def _(b):
-        for h in range(2):
-            rows = pl.ds(h * half, half)
-            sc = lax.dot_general(q[rows, :], kall[b], (((1,), (1,)), ((), ())),
-                                 preferred_element_type=jnp.float32) * inv_root
-            old = m_ref[rows, :]
-            mx = jnp.maximum(old, jnp.max(sc, axis=1, keepdims=True))
-            ex = jnp.exp(sc - mx)
-            fade = jnp.exp(old - mx)
-            m_ref[rows, :] = mx
-            l_ref[rows, :] = l_ref[rows, :] * fade + jnp.sum(ex, axis=1, keepdims=True)
-            acc_ref[rows, :] = acc_ref[rows, :] * fade + jnp.dot(
-                ex.astype(jnp.bfloat16), vall[b], preferred_element_type=jnp.float32)
+            at_distance(e - 2, relay)
+
+        @pl.when(e >= D - 1)
+        def _():
+            earlier_keys(e - (D - 1))
 
     att[...] = (acc_ref[...] / l_ref[...]).astype(jnp.bfloat16)
 
-    def pass_plane(plane):
-        @pl.loop(1, G)
-        def _(o):
-            src = (g + o) % G
-            x_copy(plane, src, g).wait_recv()
-            s_copy(plane, src, k).start()
-
-    pass_plane(d)
-
-    @pl.loop(1, D)
+    @pl.loop(0, D)
     def _(e):
-        for side in (1, 0):
-            src = d - e if side else d + e
-
-            @pl.when((src >= 0) if side else (src < D))
-            def _():
-                pass_plane(src)
+        at_distance(e, finish)
 
     @pl.loop(0, D)
     def _(plane):
@@ -311,9 +384,17 @@
 
     @pl.loop(0, D)
     def _(plane):
-        @pl.loop(1, G)
-        def _(o):
-            x_copy(plane, g, (g + o) % G).wait_send()
+        if has_x:
+            for h in (0, 1):
+                x_own(plane, h, gxn).wait_send()
+
+        @pl.loop(1, high)
+        def _(o):
+            for h in (0, 1):
+                x_own(plane, h, up(o)).wait_send()
+            if has_x:
+                x_fwd0(plane, up(o)).wait_send()
+                x_fwd1(plane, up(o)).wait_send()
 
         @pl.loop(0, G)
         def _(src):
@@ -342,7 +423,7 @@
     pool_here, tile_len, wide = encoded.shape
     rows_here = pool_here * tile_len
     rows_g = rows_here // G
-    unit = math.gcd(rows_g, tile_len)
+    unit = math.gcd(rows_g // 2, tile_len)
     spans_here = owners.shape[0]
     span_len = T // spans_here
     w = jnp.transpose(cross_kv_weight, (1, 0, 2))
@@ -375,7 +456,7 @@
             pltpu.VMEM((T, 1), f32),
             pltpu.VMEM((T, HS), f32),
             dma, dma((2,)), dma((2,)), dma((2,)), dma((2, D)), dma((D,)), dma((D,)), dma((D,)),
-            dma((D, G)), dma((D, G)), dma((D, G)), dma((D, G)),
+            dma((D, 2, G)), dma((D, 2, G)), dma((D, 2, G)), dma((D, G)), dma((D, G)),
             dma((2, G)), dma((2, G)), dma((2, G)), dma((2, G)),
         ],
         compiler_params=pltpu.CompilerParams(

time: 53.4 us -> 54.5 us (1.021)
  Pallas kernels: 47.5 us -> 48.4 us
    pallas_call x1, Pallas kernels: 47.5 us -> 48.4 us  [on_device(): pl.pallas_call(functools.partial(kernel, S, D, tile_len, 1.0 / math.sqrt(...]
where the time goes in v3:
time: 54.5 us; the launch traced here: 54.1 us
  Pallas kernels  48.4 us (89%)
  local copies, waits for them, and re-layouts  4.98 us (9%)
  between operations  0.64 us (1%)
    pallas_call x1, Pallas kernels, on_device(): pl.pallas_call(functools.partial(kernel, S, D, tile_len, 1.0 / math.sqrt(...  48.4 us
    unnamed x3, local copies, waits for them, and re-layouts  4.98 us

profile of v3, /device:TPU:1, one launch (start us, length us, event | category | flops | bytes accessed | tf_op | source)
XLA Modules:
  0.0 54.1 jit_solution(9928051397423443342)
XLA Ops:
  0.6 1.8 %copy.12 = bf16[896,2,128]{2,0,1:T(8,128)(2,1)} copy(bf16[896,2,128]{2,1,0:T(2,128)(2,1)} %param.13) | data formatting | bytes 917504 | tf_op args[5]
  2.5 48.4 %retro.1 = (bf16[512,128]{1,0:T(8,128)(2,1)}, bf16[512,128]{1,0:T(8,128)(2,1)}) custom-call(s32[2,8]{1,0:T(2,128)} %bitcast.8, s32[2,8]{1,0:T(2,128)} %bitcast.10, s32[2,8]{1,0:T(2,128)} %bitcast.9, s32[2,8]{1,0:T(2,128)} %bitcast.11, bf16[512,128]{1,0:T(8,128)(2,1)} %q.1, bf16[512,128]{1,0:T(8,128)(2,1)} %key.1, bf16[512,128]{1,0:T(8,128)(2,1)} %val.1, ...), custom_call_target="tpu_custom_call" | custom-call | tf_op jit(solution)/shard_map/retro/pallas_call | solution.py:435
  50.9 1.6 %copy.15 = bf16[512,128]{1,0:T(8,128)(2,1)} copy(bf16[512,128]{1,0:T(8,128)(2,1)} %get-tuple-element.4) | data formatting | bytes 262144
  52.5 1.6 %copy.16 = bf16[512,128]{1,0:T(8,128)(2,1)} copy(bf16[512,128]{1,0:T(8,128)(2,1)} %get-tuple-element.5) | data formatting | bytes 262144

commit v4 on v3

--- a/solution.py
+++ b/solution.py
@@ -77,14 +77,19 @@
     def block(plane, group):
         return pl.ds((plane * G + group) * units_g, units_g)
 
-    def w_own(side):
-        return pltpu.make_async_remote_copy(
-            w.at[k], wall.at[d], send_w.at[side, d], recv_w.at[d],
+    pieces = recv_w.shape[1]
+    piece = w.shape[1] // pieces
+
+    def w_own(side, c):
+        rows = pl.ds(c * piece, piece)
+        return pltpu.make_async_remote_copy(
+            w.at[k, rows], wall.at[d, rows], send_w.at[side, d, c], recv_w.at[d, c],
             device_id={"dp": d + (1 if side else -1)}, device_id_type=MESH)
 
-    def w_pass(src, side):
-        return pltpu.make_async_remote_copy(
-            wall.at[src], wall.at[src], send_w.at[side, src], recv_w.at[src],
+    def w_pass(src, side, c):
+        rows = pl.ds(c * piece, piece)
+        return pltpu.make_async_remote_copy(
+            wall.at[src, rows], wall.at[src, rows], send_w.at[side, src, c], recv_w.at[src, c],
             device_id={"dp": d + (1 if side else -1)}, device_id_type=MESH)
 
     def p_copy(to, src):
@@ -138,10 +143,11 @@
             src_ref, land.at[src * C + kk], send_ks.at[i, src], recv_ks.at[i, src],
             device_id={"seq": sib}, device_id_type=MESH)
 
-    for side in (0, 1):
-        @pl.when((d + 1 < D) if side else (d > 0))
-        def _():
-            w_own(side).start()
+    for c in range(pieces):
+        for side in (0, 1):
+            @pl.when((d + 1 < D) if side else (d > 0))
+            def _():
+                w_own(side, c).start()
 
     for i, ref in ((0, own_h), (1, row_h)):
         id_copy(i, ref).start()
@@ -280,16 +286,17 @@
     def _(e):
         @pl.when(e < D)
         def _():
-            for side in (1, 0):
-                src = d - e if side else d + e
-
-                @pl.when((src >= 0) if side else (src < D))
-                def _():
-                    w_pass(src, side).wait_recv()
-
-                    @pl.when((d + 1 < D) if side else (d > 0))
+            for c in range(pieces):
+                for side in (1, 0):
+                    src = d - e if side else d + e
+
+                    @pl.when((src >= 0) if side else (src < D))
                     def _():
-                        w_pass(src, side).start()
+                        w_pass(src, side, c).wait_recv()
+
+                        @pl.when((d + 1 < D) if side else (d > 0))
+                        def _():
+                            w_pass(src, side, c).start()
 
             for side in (1, 0):
                 src = d - e if side else d + e
@@ -370,13 +377,15 @@
     for side in (0, 1):
         @pl.when((d + 1 < D) if side else (d > 0))
         def _():
-            w_own(side).wait_send()
+            for c in range(pieces):
+                w_own(side, c).wait_send()
 
             @pl.loop(0, D)
             def _(src):
                 @pl.when((src < d) if side else (src > d))
                 def _():
-                    w_pass(src, side).wait_send()
+                    for c in range(pieces):
+                        w_pass(src, side, c).wait_send()
 
     @pl.loop(1, D)
     def _(o):
@@ -429,6 +438,7 @@
     w = jnp.transpose(cross_kv_weight, (1, 0, 2))
     own, row = owners.T, tile_rows.T
     near = own.shape[0]
+    pieces = 4 if wide % 64 == 0 else 1
     bf, f32 = jnp.bfloat16, jnp.float32
     vm = pl.BlockSpec(memory_space=pltpu.VMEM)
     dma = pltpu.SemaphoreType.DMA
@@ -455,7 +465,7 @@
             pltpu.VMEM((T, 1), f32),
             pltpu.VMEM((T, 1), f32),
             pltpu.VMEM((T, HS), f32),
-            dma, dma((2,)), dma((2,)), dma((2,)), dma((2, D)), dma((D,)), dma((D,)), dma((D,)),
+            dma, dma((2,)), dma((2,)), dma((2,)), dma((2, D, pieces)), dma((D, pieces)), dma((D,)), dma((D,)),
             dma((D, 2, G)), dma((D, 2, G)), dma((D, 2, G)), dma((D, G)), dma((D, G)),
             dma((2, G)), dma((2, G)), dma((2, G)), dma((2, G)),
         ],

time: 54.5 us -> 53.4 us (0.980)
  Pallas kernels: 48.4 us -> 47.5 us
    pallas_call x1, Pallas kernels: 48.4 us -> 47.5 us  [on_device(): pl.pallas_call(functools.partial(kernel, S, D, tile_len, 1.0 / math.sqrt(...]
where the time goes in v4:
time: 53.4 us; the launch traced here: 53.2 us
  Pallas kernels  47.5 us (89%)
  local copies, waits for them, and re-layouts  4.98 us (9%)
  between operations  0.64 us (1%)
    pallas_call x1, Pallas kernels, on_device(): pl.pallas_call(functools.partial(kernel, S, D, tile_len, 1.0 / math.sqrt(...  47.5 us
    unnamed x3, local copies, waits for them, and re-layouts  4.98 us

profile of v4, /device:TPU:1, one launch (start us, length us, event | category | flops | bytes accessed | tf_op | source)
XLA Modules:
  0.0 53.2 jit_solution(7957276238468435459)
XLA Ops:
  0.6 1.8 %copy.12 = bf16[896,2,128]{2,0,1:T(8,128)(2,1)} copy(bf16[896,2,128]{2,1,0:T(2,128)(2,1)} %param.13) | data formatting | bytes 917504 | tf_op args[5]
  2.5 47.5 %retro.1 = (bf16[512,128]{1,0:T(8,128)(2,1)}, bf16[512,128]{1,0:T(8,128)(2,1)}) custom-call(s32[2,8]{1,0:T(2,128)} %bitcast.8, s32[2,8]{1,0:T(2,128)} %bitcast.10, s32[2,8]{1,0:T(2,128)} %bitcast.9, s32[2,8]{1,0:T(2,128)} %bitcast.11, bf16[512,128]{1,0:T(8,128)(2,1)} %q.1, bf16[512,128]{1,0:T(8,128)(2,1)} %key.1, bf16[512,128]{1,0:T(8,128)(2,1)} %val.1, ...), custom_call_target="tpu_custom_call" | custom-call | tf_op jit(solution)/shard_map/retro/pallas_call | solution.py:445
  50.0 1.6 %copy.15 = bf16[512,128]{1,0:T(8,128)(2,1)} copy(bf16[512,128]{1,0:T(8,128)(2,1)} %get-tuple-element.4) | data formatting | bytes 262144
  51.6 1.6 %copy.16 = bf16[512,128]{1,0:T(8,128)(2,1)} copy(bf16[512,128]{1,0:T(8,128)(2,1)} %get-tuple-element.5) | data formatting | bytes 262144

commit v5 on v4

--- a/solution.py
+++ b/solution.py
@@ -92,9 +92,13 @@
             wall.at[src, rows], wall.at[src, rows], send_w.at[side, src, c], recv_w.at[src, c],
             device_id={"dp": d + (1 if side else -1)}, device_id_type=MESH)
 
-    def p_copy(to, src):
-        return pltpu.make_async_remote_copy(
-            pbuf.at[to], pool.at[k, block(src, g)], send_p.at[to], recv_p.at[src],
+    half_u = units_g // 2
+
+    def p_copy(to, src, h):
+        return pltpu.make_async_remote_copy(
+            pbuf.at[to, pl.ds(h * half_u, half_u)],
+            pool.at[k, pl.ds((src * G + g) * units_g + h * half_u, half_u)],
+            send_p.at[to, h], recv_p.at[src, h],
             device_id={"dp": to}, device_id_type=MESH)
 
     wide_x = 2 if G % 2 == 0 else 1
@@ -102,7 +106,6 @@
     gy, gx = g // wide_x, g % wide_x
     has_x = wide_x == 2
     gxn = gy * wide_x + (1 - gx) if has_x else g
-    half_u = units_g // 2
 
     def up(o):
         return ((gy + o) % high) * wide_x + gx
@@ -165,20 +168,15 @@
     def project(weight):
         return jnp.dot(encv[...], weight, preferred_element_type=jnp.float32).astype(jnp.bfloat16)
 
-    def spread(plane):
-        if has_x:
-            x_own(plane, 0, gxn).start()
-
-        @pl.loop(1, high)
-        def _(o):
-            x_own(plane, 1, up(o)).start()
-
-        if has_x:
-            x_own(plane, 1, gxn).start()
-
-        @pl.loop(1, high)
-        def _(o):
-            x_own(plane, 0, up(o)).start()
+    def spread(plane, ready):
+        for h in (0, 1):
+            ready(h)
+            if has_x:
+                x_own(plane, h, gxn).start()
+
+            @pl.loop(1, high)
+            def _(o):
+                x_own(plane, h, up(o)).start()
 
         s_copy(plane, g, k).start()
 
@@ -228,7 +226,7 @@
 
     enc_copy.wait()
     pool[k, block(d, g)] = project(w[k]).reshape(units_g, unit, HS)
-    spread(d)
+    spread(d, lambda h: None)
 
     shifted = jnp.concatenate(
         [cq[...].astype(jnp.float32), jnp.zeros((span_len, HS), jnp.float32)], axis=0)
@@ -304,7 +302,8 @@
                 @pl.when((src >= 0) if side else (src < D))
                 def _():
                     pbuf[src] = project(wall[src]).reshape(units_g, unit, HS)
-                    p_copy(src, d).start()
+                    for h in (0, 1):
+                        p_copy(src, d, h).start()
 
         @pl.when(e == D - 1)
         def _():
@@ -317,8 +316,7 @@
         @pl.when((e > 1) & (e <= D))
         def _():
             def arrive(src):
-                p_copy(d, src).wait_recv()
-                spread(src)
+                spread(src, lambda h: p_copy(d, src, h).wait_recv())
 
             at_distance(e - 1, arrive)
 
@@ -389,7 +387,8 @@
 
     @pl.loop(1, D)
     def _(o):
-        p_copy((d + o) % D, d).wait_send()
+        for h in (0, 1):
+            p_copy((d + o) % D, d, h).wait_send()
 
     @pl.loop(0, D)
     def _(plane):
@@ -465,7 +464,7 @@
             pltpu.VMEM((T, 1), f32),
             pltpu.VMEM((T, 1), f32),
             pltpu.VMEM((T, HS), f32),
-            dma, dma((2,)), dma((2,)), dma((2,)), dma((2, D, pieces)), dma((D, pieces)), dma((D,)), dma((D,)),
+            dma, dma((2,)), dma((2,)), dma((2,)), dma((2, D, pieces)), dma((D, pieces)), dma((D, 2)), dma((D, 2)),
             dma((D, 2, G)), dma((D, 2, G)), dma((D, 2, G)), dma((D, G)), dma((D, G)),
             dma((2, G)), dma((2, G)), dma((2, G)), dma((2, G)),
         ],

time: 53.4 us -> 54.4 us (1.019)
  Pallas kernels: 47.5 us -> 48.5 us
    pallas_call x1, Pallas kernels: 47.5 us -> 48.5 us  [on_device(): pl.pallas_call(functools.partial(kernel, S, D, tile_len, 1.0 / math.sqrt(...]
where the time goes in v5:
time: 54.4 us; the launch traced here: 54.2 us
  Pallas kernels  48.5 us (89%)
  local copies, waits for them, and re-layouts  4.98 us (9%)
  between operations  0.64 us (1%)
    pallas_call x1, Pallas kernels, on_device(): pl.pallas_call(functools.partial(kernel, S, D, tile_len, 1.0 / math.sqrt(...  48.5 us
    unnamed x3, local copies, waits for them, and re-layouts  4.98 us

profile of v5, /device:TPU:1, one launch (start us, length us, event | category | flops | bytes accessed | tf_op | source)
XLA Modules:
  0.0 54.2 jit_solution(6039446325512830826)
XLA Ops:
  0.6 1.8 %copy.12 = bf16[896,2,128]{2,0,1:T(8,128)(2,1)} copy(bf16[896,2,128]{2,1,0:T(2,128)(2,1)} %param.13) | data formatting | bytes 917504 | tf_op args[5]
  2.5 48.5 %retro.1 = (bf16[512,128]{1,0:T(8,128)(2,1)}, bf16[512,128]{1,0:T(8,128)(2,1)}) custom-call(s32[2,8]{1,0:T(2,128)} %bitcast.8, s32[2,8]{1,0:T(2,128)} %bitcast.10, s32[2,8]{1,0:T(2,128)} %bitcast.9, s32[2,8]{1,0:T(2,128)} %bitcast.11, bf16[512,128]{1,0:T(8,128)(2,1)} %q.1, bf16[512,128]{1,0:T(8,128)(2,1)} %key.1, bf16[512,128]{1,0:T(8,128)(2,1)} %val.1, ...), custom_call_target="tpu_custom_call" | custom-call | tf_op jit(solution)/shard_map/retro/pallas_call | solution.py:444
  51.0 1.6 %copy.15 = bf16[512,128]{1,0:T(8,128)(2,1)} copy(bf16[512,128]{1,0:T(8,128)(2,1)} %get-tuple-element.4) | data formatting | bytes 262144
  52.6 1.6 %copy.16 = bf16[512,128]{1,0:T(8,128)(2,1)} copy(bf16[512,128]{1,0:T(8,128)(2,1)} %get-tuple-element.5) | data formatting | bytes 262144

commit v6 on v2

--- a/solution.py
+++ b/solution.py
@@ -77,14 +77,19 @@
     def block(plane, group):
         return pl.ds((plane * G + group) * units_g, units_g)
 
-    def w_own(side):
-        return pltpu.make_async_remote_copy(
-            w.at[k], wall.at[d], send_w.at[side, d], recv_w.at[d],
+    pieces = recv_w.shape[1]
+    piece = w.shape[1] // pieces
+
+    def w_own(side, c):
+        rows = pl.ds(c * piece, piece)
+        return pltpu.make_async_remote_copy(
+            w.at[k, rows], wall.at[d, rows], send_w.at[side, d, c], recv_w.at[d, c],
             device_id={"dp": d + (1 if side else -1)}, device_id_type=MESH)
 
-    def w_pass(src, side):
-        return pltpu.make_async_remote_copy(
-            wall.at[src], wall.at[src], send_w.at[side, src], recv_w.at[src],
+    def w_pass(src, side, c):
+        rows = pl.ds(c * piece, piece)
+        return pltpu.make_async_remote_copy(
+            wall.at[src, rows], wall.at[src, rows], send_w.at[side, src, c], recv_w.at[src, c],
             device_id={"dp": d + (1 if side else -1)}, device_id_type=MESH)
 
     def p_copy(to, src):
@@ -116,10 +121,11 @@
             src_ref, land.at[src * C + kk], send_ks.at[i, src], recv_ks.at[i, src],
             device_id={"seq": sib}, device_id_type=MESH)
 
-    for side in (0, 1):
-        @pl.when((d + 1 < D) if side else (d > 0))
-        def _():
-            w_own(side).start()
+    for c in range(pieces):
+        for side in (0, 1):
+            @pl.when((d + 1 < D) if side else (d > 0))
+            def _():
+                w_own(side, c).start()
 
     for i, ref in ((0, own_h), (1, row_h)):
         id_copy(i, ref).start()
@@ -174,16 +180,17 @@
     def _(e):
         @pl.when(e < D)
         def _():
-            for side in (1, 0):
-                src = d - e if side else d + e
-
-                @pl.when((src >= 0) if side else (src < D))
-                def _():
-                    w_pass(src, side).wait_recv()
-
-                    @pl.when((d + 1 < D) if side else (d > 0))
+            for c in range(pieces):
+                for side in (1, 0):
+                    src = d - e if side else d + e
+
+                    @pl.when((src >= 0) if side else (src < D))
                     def _():
-                        w_pass(src, side).start()
+                        w_pass(src, side, c).wait_recv()
+
+                        @pl.when((d + 1 < D) if side else (d > 0))
+                        def _():
+                            w_pass(src, side, c).start()
 
             for side in (1, 0):
                 src = d - e if side else d + e
@@ -297,13 +304,15 @@
     for side in (0, 1):
         @pl.when((d + 1 < D) if side else (d > 0))
         def _():
-            w_own(side).wait_send()
+            for c in range(pieces):
+                w_own(side, c).wait_send()
 
             @pl.loop(0, D)
             def _(src):
                 @pl.when((src < d) if side else (src > d))
                 def _():
-                    w_pass(src, side).wait_send()
+                    for c in range(pieces):
+                        w_pass(src, side, c).wait_send()
 
     @pl.loop(1, D)
     def _(o):
@@ -348,6 +357,7 @@
     w = jnp.transpose(cross_kv_weight, (1, 0, 2))
     own, row = owners.T, tile_rows.T
     near = own.shape[0]
+    pieces = 4 if wide % 64 == 0 else 1
     bf, f32 = jnp.bfloat16, jnp.float32
     vm = pl.BlockSpec(memory_space=pltpu.VMEM)
     dma = pltpu.SemaphoreType.DMA
@@ -374,7 +384,7 @@
             pltpu.VMEM((T, 1), f32),
             pltpu.VMEM((T, 1), f32),
             pltpu.VMEM((T, HS), f32),
-            dma, dma((2,)), dma((2,)), dma((2,)), dma((2, D)), dma((D,)), dma((D,)), dma((D,)),
+            dma, dma((2,)), dma((2,)), dma((2,)), dma((2, D, pieces)), dma((D, pieces)), dma((D,)), dma((D,)),
             dma((D, G)), dma((D, G)), dma((D, G)), dma((D, G)),
             dma((2, G)), dma((2, G)), dma((2, G)), dma((2, G)),
         ],

time: 53.4 us -> 53.4 us (level)
  no operation moved by 1% of the time
where the time goes in v6:
time: 53.4 us; the launch traced here: 53.2 us
  Pallas kernels  47.5 us (89%)
  local copies, waits for them, and re-layouts  4.98 us (9%)
  between operations  0.64 us (1%)
    pallas_call x1, Pallas kernels, on_device(): pl.pallas_call(functools.partial(kernel, S, D, tile_len, 1.0 / math.sqrt(...  47.5 us
    unnamed x3, local copies, waits for them, and re-layouts  4.98 us

profile of v6, /device:TPU:1, one launch (start us, length us, event | category | flops | bytes accessed | tf_op | source)
XLA Modules:
  0.0 53.2 jit_solution(15767795430436227102)
XLA Ops:
  0.6 1.8 %copy.12 = bf16[896,2,128]{2,0,1:T(8,128)(2,1)} copy(bf16[896,2,128]{2,1,0:T(2,128)(2,1)} %param.13) | data formatting | bytes 917504 | tf_op args[5]
  2.5 47.5 %retro.1 = (bf16[512,128]{1,0:T(8,128)(2,1)}, bf16[512,128]{1,0:T(8,128)(2,1)}) custom-call(s32[2,8]{1,0:T(2,128)} %bitcast.8, s32[2,8]{1,0:T(2,128)} %bitcast.10, s32[2,8]{1,0:T(2,128)} %bitcast.9, s32[2,8]{1,0:T(2,128)} %bitcast.11, bf16[512,128]{1,0:T(8,128)(2,1)} %q.1, bf16[512,128]{1,0:T(8,128)(2,1)} %key.1, bf16[512,128]{1,0:T(8,128)(2,1)} %val.1, ...), custom_call_target="tpu_custom_call" | custom-call | tf_op jit(solution)/shard_map/retro/pallas_call | solution.py:364
  50.0 1.6 %copy.15 = bf16[512,128]{1,0:T(8,128)(2,1)} copy(bf16[512,128]{1,0:T(8,128)(2,1)} %get-tuple-element.4) | data formatting | bytes 262144
  51.6 1.6 %copy.16 = bf16[512,128]{1,0:T(8,128)(2,1)} copy(bf16[512,128]{1,0:T(8,128)(2,1)} %get-tuple-element.5) | data formatting | bytes 262144
